TPU v7x, 32 devices: a whole 2x2x4 slice. The times are simulated.
32 devices in a mesh: energy: 8 (over y, x, core), space: 4 (over z).
Axes of the slice: x: 2, y: 2, z: 4, core: 2. Of those that a mesh axis runs over, the one named last changes fastest.
Arguments:
- green: bfloat16 [4, 8, 4, 384, 384], P(None, 'energy', 'space'), may hold values from -6 to 6
- v_diag: bfloat16 [4, 384, 384], P('space'), may hold values from -0.3125 to 0.3125
- v_low: bfloat16 [4, 384, 384], P('space'), may hold values from -0.3125 to 0.3125
- energy_slot: int32 [8], replicated, may hold values from 0 to 7, each once
Outputs:
- sigma: bfloat16 [2, 8, 4, 384, 384], P(None, None, 'space', 'energy')
Inputs may be any that keep to these rules, and one draw needn't show every extreme that they name: `energy_slot`: each grid energy appears in exactly one slot.
All inputs are finite; a program needn't handle non-finite values.
Results may differ from a plain program's by a relative error of at most 0.0066.
Values may be sent and summed in bfloat16 or wider, within the bound.
No kernel may reach another device: no remote copies, remote signals or barrier semaphores. Data moves between devices by JAX's collectives and lax.ppermute only.
A program may use at most 64 MiB of HBM per device.

v0:
```python
import math
import jax
import jax.numpy as jnp
from jax import lax
from jax.sharding import PartitionSpec as P


def shifted(value, axis, steps):
    count = lax.axis_size(axis)
    leading, last = (max(0, -steps), min(count, count - steps))
    return lax.ppermute(value, axis, [(source, source + steps) for source in range(leading, last)])


def apply_table(table, values):
    return jnp.dot(
        table, values, precision=lax.Precision.HIGHEST, preferred_element_type=jnp.float32
    )


def spectra(cos_table, sin_table, real_part, imag_part):
    out_real = apply_table(cos_table, real_part) + apply_table(sin_table, imag_part)
    out_imag = apply_table(cos_table, imag_part) - apply_table(sin_table, real_part)
    return (out_real, out_imag)


def to_slots(cos_table, sin_table, real_part, imag_part):
    factor = 1.0 / cos_table.shape[0]
    cos_back = cos_table.T
    sin_back = sin_table.T
    out_real = (apply_table(cos_back, real_part) - apply_table(sin_back, imag_part)) * factor
    out_imag = (apply_table(cos_back, imag_part) + apply_table(sin_back, real_part)) * factor
    return (out_real, out_imag)


def sandwich(matrix, polar):
    left = jnp.einsum("ij,cejk->ceik", matrix, polar, preferred_element_type=jnp.float32).astype(
        jnp.bfloat16
    )
    return jnp.einsum("ceij,kj->ceik", left, matrix, preferred_element_type=jnp.float32)


def sandwich_t(matrix, polar):
    left = jnp.einsum("ji,cejk->ceik", matrix, polar, preferred_element_type=jnp.float32).astype(
        jnp.bfloat16
    )
    return jnp.einsum("ceij,jk->ceik", left, matrix, preferred_element_type=jnp.float32)


def shards(green, v_diag, v_low, energy_slot):
    energies = energy_slot.shape[0]
    period = 2 * energies
    frequency = jnp.arange(period, dtype=jnp.int32)
    phases = frequency[:, None] * energy_slot[None, :] % period
    angles = phases.astype(jnp.float32) * (2.0 * math.pi / period)
    cos_table = jnp.cos(angles)
    sin_table = jnp.sin(angles)
    scaling = energies ** (-0.5)
    arrived = lax.all_to_all(green[:, :, 0], "energy", split_axis=2, concat_axis=1, tiled=True)
    row_count = arrived.shape[2]
    col_count = arrived.shape[3]
    flattened = arrived.reshape((4, energies, row_count * col_count)).astype(jnp.float32)
    lesser_re, lesser_im = spectra(cos_table, sin_table, flattened[0], flattened[1])
    greater_re, greater_im = spectra(cos_table, sin_table, flattened[2], flattened[3])
    cross_re = lesser_re * greater_re + lesser_im * greater_im
    cross_im = lesser_im * greater_re - lesser_re * greater_im
    corr_re, corr_im = to_slots(cos_table, sin_table, cross_re, cross_im)
    polar_slot = (
        jnp.stack([corr_im * scaling, -corr_re * scaling])
        .reshape((2, energies, row_count, col_count))
        .astype(jnp.bfloat16)
    )
    polar = lax.all_to_all(polar_slot, "energy", split_axis=1, concat_axis=2, tiled=True)
    diagonal = v_diag[0]
    lower = v_low[0]
    own_term = sandwich(diagonal, polar)
    below = shifted(polar, "space", 1)
    handed = sandwich_t(lower, polar).astype(jnp.bfloat16)
    received = shifted(handed, "space", -1)
    total = own_term + sandwich(lower, below) + received.astype(jnp.float32)
    screened = total.astype(jnp.bfloat16)
    screened_rows = lax.all_to_all(screened, "energy", split_axis=2, concat_axis=1, tiled=True)
    weights = screened_rows.reshape((2, energies, row_count * col_count)).astype(jnp.float32)
    weight_re, weight_im = spectra(cos_table, sin_table, weights[0], weights[1])
    joint_re = lesser_re * weight_re - lesser_im * weight_im
    joint_im = lesser_re * weight_im + lesser_im * weight_re
    conv_re, conv_im = to_slots(cos_table, sin_table, joint_re, joint_im)
    sigma = (
        jnp.stack([-conv_im * scaling, conv_re * scaling])
        .reshape((2, energies, row_count, col_count))
        .astype(jnp.bfloat16)
    )
    return sigma[:, :, None]


def solution(mesh):
    in_specs = (
        P(None, "energy", "space", None, None),
        P("space", None, None),
        P("space", None, None),
        P(),
    )
    out_specs = P(None, None, "space", "energy", None)
    return jax.shard_map(shards, mesh=mesh, in_specs=in_specs, out_specs=out_specs, check_vma=False)
```

profile of v0, /device:TPU:24, one launch (start us, length us, event | category | flops | bytes accessed | tf_op | source)
XLA Modules:
  0.0 103.2 jit_solution(476986298993754648)
XLA Ops:
  0.0 2.2 %copy.56 = bf16[4,1,1,384,384]{4,0,3,2,1:T(4,128)(2,1)S(1)} copy(bf16[4,1,1,384,384]{4,3,2,1,0:T(8,128)(2,1)} %param.4) | data formatting | bytes 2359296 | tf_op args[0]
  2.2 20.3 %all_to_all.30 = bf16[4,1,384,384]{3,0,1,2:T(4,128)(2,1)S(1)} all-to-all(bf16[4,1,384,384]{3,0,1,2:T(4,128)(2,1)S(1)} %bitcast.85), channel_id=1, replica_groups=mesh['energy'=8,'space'=4] {'energy'}, dimensions={2} | all-to-all | bytes 2359296 | tf_op jit(solution)/shard_map/all_to_all | solution.py:58
  22.5 7.5 %slice_reduce_fusion.3 = (bf16[384,384]{1,0:T(8,128)(2,1)S(1)}, bf16[384,384]{1,0:T(8,128)(2,1)S(1)}, bf16[384,384]{1,0:T(8,128)(2,1)S(1)}, bf16[384,384]{1,0:T(8,128)(2,1)S(1)}) fusion(bf16[4,1,384,384]{3,0,1,2:T(4,128)(2,1)S(1)} %all_to_all.30), kind=kLoop, calls=%fused_computation.42 | loop fusion | bytes 2359296 | tf_op jit(solution)/shard_map/slice | solution.py:63
  35.4 2.1 %multiply_subtract_fusion.1 = (f32[16,18432]{1,0:T(8,128)S(1)}, f32[16,18432]{1,0:T(8,128)S(1)}, f32[16,18432]{1,0:T(8,128)}) fusion(f32[16,18432]{1,0:T(8,128)S(1)} %convolution_subtract_fusion.1, f32[16,18432]{1,0:T(8,128)S(1)} %convolution_subtract_fusion.2, f32[16,18432]{1,0:T(8,128)S(1)} %convolution_add_fusion.1, f32[16,18432]{1,0:T(8,128)S(1)} %fusion.52, ...), kind=kOutput, calls=%fused_computation.38 | convolution fusion | flops 30377728 | bytes 8552480 | tf_op jit(solution)/shard_map/dot_general | solution.py:15
  37.4 0.7 fusion.44
  38.9 0.8 fusion.8
  39.7 0.8 fusion.9
  40.6 12.8 %all_to_all.31 = bf16[2,8,48,384]{3,2,0,1:T(8,128)(2,1)S(1)} all-to-all(bf16[2,8,48,384]{3,2,0,1:T(8,128)(2,1)S(1)} %pad_maximum_fusion), channel_id=1, replica_groups=mesh['energy'=8,'space'=4] {'energy'}, dimensions={1} | all-to-all | bytes 1179648 | tf_op jit(solution)/shard_map/all_to_all | solution.py:72
  53.5 1.1 %copy.43 = bf16[2,1,384,384]{2,3,0,1:T(8,128)(2,1)} copy(bf16[2,1,384,384]{3,2,0,1:T(8,128)(2,1)S(1)} %bitcast.82) | data formatting | bytes 1179648 | tf_op jit(solution)/shard_map/all_to_all | solution.py:72
  54.6 1.9 %fusion.17 = bf16[2,1,384,384]{3,2,0,1:T(8,128)(2,1)} fusion(bf16[2,384,384]{2,1,0:T(8,128)(2,1)S(1)} %bitcast.83, bf16[1,384,384]{2,1,0:T(8,128)(2,1)S(1)} %copy-done), kind=kOutput, calls=%fused_computation.32 | convolution fusion | flops 453574656 | bytes 1474560 | tf_op jit(solution)/shard_map/ceij,jk->ceik/dot_general | solution.py:46
  56.5 3.2 %collective-permute-start.1 = (bf16[2,1,384,384]{3,2,0,1:T(8,128)(2,1)}, bf16[2,1,384,384]{3,2,0,1:T(8,128)(2,1)}, u32[]{:S(2)}, u32[]{:S(2)}) collective-permute-start(bf16[2,1,384,384]{3,2,0,1:T(8,128)(2,1)} %fusion.17), channel_id=1, source_target_pairs={{1,0},{2,1},{3,2},{5,4},{6,5},{7,6},{9,8},{10,9},{11,10},{13,12},{... | collective-permute-start | bytes 1769480 | tf_op jit(solution)/shard_map/ppermute | solution.py:11
  59.7 1.5 %collective-permute-start = (bf16[2,1,384,384]{2,3,0,1:T(8,128)(2,1)}, bf16[2,1,384,384]{2,3,0,1:T(8,128)(2,1)}, u32[]{:S(2)}, u32[]{:S(2)}) collective-permute-start(bf16[2,1,384,384]{2,3,0,1:T(8,128)(2,1)} %copy.43), channel_id=1, source_target_pairs={{0,1},{1,2},{2,3},{4,5},{5,6},{6,7},{8,9},{9,10},{10,11},{12,13},{... | collective-permute-start | bytes 1769480 | tf_op jit(solution)/shard_map/ppermute | solution.py:11
  61.2 1.1 %fusion.14 = f32[2,384,384]{2,1,0:T(8,128)S(1)} fusion(bf16[2,384,384]{2,1,0:T(8,128)(2,1)S(1)} %bitcast.84, bf16[1,384,384]{2,1,0:T(8,128)(2,1)S(1)} %copy-done.2), kind=kOutput, calls=%fused_computation.29 | convolution fusion | flops 453279744 | bytes 2064384 | tf_op jit(solution)/shard_map/ceij,kj->ceik/dot_general | solution.py:39
  62.3 9.4 %collective-permute-done.1 = bf16[2,1,384,384]{3,2,0,1:T(8,128)(2,1)} collective-permute-done((bf16[2,1,384,384]{3,2,0,1:T(8,128)(2,1)}, bf16[2,1,384,384]{3,2,0,1:T(8,128)(2,1)}, u32[]{:S(2)}, u32[]{:S(2)}) %collective-permute-start.1) | collective-permute-done | bytes 589856 | tf_op jit(solution)/shard_map/ppermute | solution.py:11
  71.6 5.0 %collective-permute-done = bf16[2,1,384,384]{2,3,0,1:T(8,128)(2,1)} collective-permute-done((bf16[2,1,384,384]{2,3,0,1:T(8,128)(2,1)}, bf16[2,1,384,384]{2,3,0,1:T(8,128)(2,1)}, u32[]{:S(2)}, u32[]{:S(2)}) %collective-permute-start) | collective-permute-done | bytes 589856 | tf_op jit(solution)/shard_map/ppermute | solution.py:11
  76.6 2.3 %add_convert_fusion = bf16[2,1,384,384]{3,2,0,1:T(8,128)(2,1)S(1)} fusion(bf16[2,1,384,384]{3,2,0,1:T(8,128)(2,1)} %collective-permute-done.1, f32[2,384,384]{2,1,0:T(8,128)S(1)} %fusion.14, bf16[2,1,384,384]{2,3,0,1:T(8,128)(2,1)} %collective-permute-done, bf16[1,384,384]{2,1,0:T(8,128)(2,1)S(1)} %copy-done), kind=kOutput, calls=%fused_computation.36 | convolution fusion | flops 454459392 | bytes 3244032 | tf_op jit(solution)/shard_map/ceij,kj->ceik/dot_general | solution.py:39
  79.5 12.8 %all_to_all.32 = bf16[2,1,384,384]{3,0,1,2:T(2,128)(2,1)S(1)} all-to-all(bf16[2,1,384,384]{3,0,1,2:T(2,128)(2,1)S(1)} %copy.47), channel_id=1, replica_groups=mesh['energy'=8,'space'=4] {'energy'}, dimensions={2} | all-to-all | bytes 1179648 | tf_op jit(solution)/shard_map/all_to_all | solution.py:81
  92.3 2.9 %slice_reduce_fusion = (bf16[384,384]{1,0:T(8,128)(2,1)S(1)}, bf16[384,384]{1,0:T(8,128)(2,1)S(1)}) fusion(bf16[2,1,384,384]{3,0,1,2:T(2,128)(2,1)S(1)} %all_to_all.32), kind=kLoop, calls=%fused_computation.39 | loop fusion | bytes 1179648 | tf_op jit(solution)/shard_map/slice | solution.py:83
  98.1 1.0 %multiply_add_fusion = (f32[16,18432]{1,0:T(8,128)S(1)}, f32[16,18432]{1,0:T(8,128)S(1)}) fusion(f32[16,18432]{1,0:T(8,128)S(1)} %convolution_subtract_fusion.2, f32[16,18432]{1,0:T(8,128)S(1)} %copy-done.1, f32[16,18432]{1,0:T(8,128)S(1)} %convolution_subtract_fusion, f32[16,18432]{1,0:T(8,128)S(1)} %fusion.38, bf16[8,18432]{1,0:T(8,128)(2,1)S(1)} %squeeze.34, ...), kind=kOutput, calls=%fused_computation.35 | convolution fusion | flops 30377728 | bytes 7372832 | tf_op jit(solution)/shard_map/dot_general | solution.py:15
  99.2 0.7 fusion.36
  99.9 0.7 fusion.34
  100.7 0.8 fusion.10
  101.5 0.7 fusion.11
  102.3 0.9 pad_maximum_fusion.1
  (32 shorter events, 9.7 us)
Async XLA Ops:
  0.0 54.6 %copy-start = (bf16[1,384,384]{2,1,0:T(8,128)(2,1)S(1)}, bf16[1,384,384]{2,1,0:T(8,128)(2,1)}, u32[]{:S(2)}) copy-start(bf16[1,384,384]{2,1,0:T(8,128)(2,1)} %param.6) | copy-start | bytes 884740
  30.0 0.7 copy-start.3
  54.6 6.6 %copy-start.2 = (bf16[1,384,384]{2,1,0:T(8,128)(2,1)S(1)}, bf16[1,384,384]{2,1,0:T(8,128)(2,1)}, u32[]{:S(2)}) copy-start(bf16[1,384,384]{2,1,0:T(8,128)(2,1)} %param.5) | copy-start | bytes 884740
  56.5 15.2 %collective-permute-start.1 = (bf16[2,1,384,384]{3,2,0,1:T(8,128)(2,1)}, bf16[2,1,384,384]{3,2,0,1:T(8,128)(2,1)}, u32[]{:S(2)}, u32[]{:S(2)}) collective-permute-start(bf16[2,1,384,384]{3,2,0,1:T(8,128)(2,1)} %fusion.17), channel_id=1, source_target_pairs={{1,0},{2,1},{3,2},{5,4},{6,5},{7,6},{9,8},{10,9},{11,10},{13,12},{... | collective-permute-start | bytes 1769480 | tf_op jit(solution)/shard_map/ppermute | solution.py:11
  59.7 16.9 %collective-permute-start = (bf16[2,1,384,384]{2,3,0,1:T(8,128)(2,1)}, bf16[2,1,384,384]{2,3,0,1:T(8,128)(2,1)}, u32[]{:S(2)}, u32[]{:S(2)}) collective-permute-start(bf16[2,1,384,384]{2,3,0,1:T(8,128)(2,1)} %copy.43), channel_id=1, source_target_pairs={{0,1},{1,2},{2,3},{4,5},{5,6},{6,7},{8,9},{9,10},{10,11},{12,13},{... | collective-permute-start | bytes 1769480 | tf_op jit(solution)/shard_map/ppermute | solution.py:11
  96.9 1.3 %copy-start.1 = (f32[16,18432]{1,0:T(8,128)S(1)}, f32[16,18432]{1,0:T(8,128)}, u32[]{:S(2)}) copy-start(f32[16,18432]{1,0:T(8,128)} %get-tuple-element.15) | copy-start | bytes 3538948
where the time goes:
time: 104 us; the launch traced here: 103 us
  blocking collectives  45.9 us (44%)
  matrix products  20.9 us (20%)
  local copies, waits for them, and re-layouts  16.1 us (15%)
  waiting for transfers between devices  14.3 us (14%)
  starting transfers between devices  4.7 us (5%)
    all_to_all x1, blocking collectives, shards(): lax.all_to_all(green[:, :, 0], 'energy', split_axis=2, concat_axis=1, til...  20.3 us
    dot_general x20, matrix products, apply_table(): jnp.dot(table, values, precision=lax.Precision.HIGHEST, preferred_element...  15.7 us
    ppermute x2, waiting for transfers between devices, shifted(): lax.ppermute(value, axis, [(source, source + steps) for source in range(l...  14.3 us
    all_to_all x1, blocking collectives, shards(): lax.all_to_all(polar_slot, 'energy', split_axis=1, concat_axis=2, tiled=T...  12.8 us
    all_to_all x1, blocking collectives, shards(): lax.all_to_all(screened, 'energy', split_axis=2, concat_axis=1, tiled=True)  12.8 us
    slice x1, local copies, waits for them, and re-layouts, shards(): flattened[2]  7.53 us
    ppermute x2, starting transfers between devices, shifted(): lax.ppermute(value, axis, [(source, source + steps) for source in range(l...  4.7 us
    dot_general x2, matrix products, sandwich(): jnp.einsum('ceij,kj->ceik', left, matrix, preferred_element_type=jnp.floa...  3.35 us
  transfers between devices with their start and end apart: 2, of which 2 were waited for; matrix products, arithmetic and copies ran while one was open for 1% of the time, Pallas kernels for 0%

commit v1 on v0

--- a/solution.py
+++ b/solution.py
@@ -47,6 +47,15 @@
 
 
 def shards(green, v_diag, v_low, energy_slot):
+
+    def mark_stages_all(block_here):
+        return jnp.concatenate(
+            lax.all_to_all(
+                jnp.stack(jnp.split(block_here, lax.axis_size("energy"), axis=2)), "energy", 0, 0
+            ),
+            axis=1,
+        )
+
     energies = energy_slot.shape[0]
     period = 2 * energies
     frequency = jnp.arange(period, dtype=jnp.int32)
@@ -55,7 +64,7 @@
     cos_table = jnp.cos(angles)
     sin_table = jnp.sin(angles)
     scaling = energies ** (-0.5)
-    arrived = lax.all_to_all(green[:, :, 0], "energy", split_axis=2, concat_axis=1, tiled=True)
+    arrived = mark_stages_all(green[:, :, 0])
     row_count = arrived.shape[2]
     col_count = arrived.shape[3]
     flattened = arrived.reshape((4, energies, row_count * col_count)).astype(jnp.float32)

time: 104 us -> 98 us (0.942)
  local copies, waits for them, and re-layouts: 16.1 us -> 10.4 us
    slice x1 -> x0, local copies, waits for them, and re-layouts: 7.53 us -> none  [shards(): flattened[2]]
    unnamed x9 -> x22, local copies, waits for them, and re-layouts: 2.88 us -> 5.28 us
where the time goes in v1:
time: 98 us; the launch traced here: 97.6 us
  blocking collectives  45.9 us (47%)
  matrix products  21 us (21%)
  waiting for transfers between devices  14.4 us (15%)
  local copies, waits for them, and re-layouts  10.4 us (11%)
  starting transfers between devices  4.66 us (5%)
    all_to_all x1, blocking collectives, mark_stages_all(): lax.all_to_all(jnp.stack(jnp.split(block_here, lax.axis_size('energy'), a...  20.3 us
    dot_general x20, matrix products, apply_table(): jnp.dot(table, values, precision=lax.Precision.HIGHEST, preferred_element...  15.7 us
    ppermute x2, waiting for transfers between devices, shifted(): lax.ppermute(value, axis, [(source, source + steps) for source in range(l...  14.4 us
    all_to_all x1, blocking collectives, shards(): lax.all_to_all(polar_slot, 'energy', split_axis=1, concat_axis=2, tiled=T...  12.8 us
    all_to_all x1, blocking collectives, shards(): lax.all_to_all(screened, 'energy', split_axis=2, concat_axis=1, tiled=True)  12.8 us
    unnamed x22, local copies, waits for them, and re-layouts  5.28 us
    ppermute x2, starting transfers between devices, shifted(): lax.ppermute(value, axis, [(source, source + steps) for source in range(l...  4.66 us
    dot_general x2, matrix products, sandwich(): jnp.einsum('ceij,kj->ceik', left, matrix, preferred_element_type=jnp.floa...  3.34 us
  transfers between devices with their start and end apart: 2, of which 2 were waited for; matrix products, arithmetic and copies ran while one was open for 1% of the time, Pallas kernels for 0%

profile of v1, /device:TPU:24, one launch (start us, length us, event | category | flops | bytes accessed | tf_op | source)
XLA Modules:
  0.0 97.6 jit_solution(14082940904769421921)
XLA Ops:
  0.0 1.0 %fusion.33 = bf16[8,4,1,48,384]{4,3,1,2,0:T(8,128)(2,1)S(1)} fusion(bf16[4,1,384,384]{3,2,0,1:T(8,128)(2,1)} %bitcast.149), kind=kLoop, calls=%fused_computation.65 | loop fusion | bytes 294912
  1.0 0.9 fusion.32
  2.0 0.9 fusion.31
  2.9 0.9 fusion.30
  4.0 20.3 %all_to_all.26 = bf16[8,4,1,48,384]{4,3,1,2,0:T(8,128)(2,1)S(1)} all-to-all(bf16[8,4,1,48,384]{4,3,1,2,0:T(8,128)(2,1)S(1)} %fusion.26), channel_id=1, replica_groups=mesh['energy'=8,'space'=4] {'energy'}, dimensions={0} | all-to-all | bytes 2359296 | tf_op jit(solution)/shard_map/all_to_all | solution.py:53
  29.7 2.1 %multiply_subtract_fusion.1 = (f32[16,18432]{1,0:T(8,128)S(1)}, f32[16,18432]{1,0:T(8,128)S(1)}, f32[16,18432]{1,0:T(8,128)}) fusion(f32[16,18432]{1,0:T(8,128)S(1)} %convolution_subtract_fusion.1, f32[16,18432]{1,0:T(8,128)S(1)} %convolution_subtract_fusion.2, f32[16,18432]{1,0:T(8,128)S(1)} %convolution_add_fusion.1, f32[16,18432]{1,0:T(8,128)S(1)} %fusion.60, ...), kind=kOutput, calls=%fused_computation.37 | convolution fusion | flops 30377728 | bytes 8552480 | tf_op jit(solution)/shard_map/dot_general | solution.py:15
  33.3 0.8 fusion.8
  34.1 0.8 fusion.9
  35.0 12.8 %all_to_all.27 = bf16[2,8,48,384]{3,2,0,1:T(8,128)(2,1)S(1)} all-to-all(bf16[2,8,48,384]{3,2,0,1:T(8,128)(2,1)S(1)} %pad_maximum_fusion), channel_id=1, replica_groups=mesh['energy'=8,'space'=4] {'energy'}, dimensions={1} | all-to-all | bytes 1179648 | tf_op jit(solution)/shard_map/all_to_all | solution.py:81
  47.9 1.1 %copy.41 = bf16[2,1,384,384]{2,3,0,1:T(8,128)(2,1)} copy(bf16[2,1,384,384]{3,2,0,1:T(8,128)(2,1)S(1)} %bitcast.133) | data formatting | bytes 1179648 | tf_op jit(solution)/shard_map/all_to_all | solution.py:81
  49.0 1.9 %fusion.17 = bf16[2,1,384,384]{3,2,0,1:T(8,128)(2,1)} fusion(bf16[2,384,384]{2,1,0:T(8,128)(2,1)S(1)} %bitcast.134, bf16[1,384,384]{2,1,0:T(8,128)(2,1)S(1)} %copy-done), kind=kOutput, calls=%fused_computation.32 | convolution fusion | flops 453574656 | bytes 1474560 | tf_op jit(solution)/shard_map/ceij,jk->ceik/dot_general | solution.py:46
  50.9 3.2 %collective-permute-start.1 = (bf16[2,1,384,384]{3,2,0,1:T(8,128)(2,1)}, bf16[2,1,384,384]{3,2,0,1:T(8,128)(2,1)}, u32[]{:S(2)}, u32[]{:S(2)}) collective-permute-start(bf16[2,1,384,384]{3,2,0,1:T(8,128)(2,1)} %fusion.17), channel_id=1, source_target_pairs={{1,0},{2,1},{3,2},{5,4},{6,5},{7,6},{9,8},{10,9},{11,10},{13,12},{... | collective-permute-start | bytes 1769480 | tf_op jit(solution)/shard_map/ppermute | solution.py:11
  54.1 1.5 %collective-permute-start = (bf16[2,1,384,384]{2,3,0,1:T(8,128)(2,1)}, bf16[2,1,384,384]{2,3,0,1:T(8,128)(2,1)}, u32[]{:S(2)}, u32[]{:S(2)}) collective-permute-start(bf16[2,1,384,384]{2,3,0,1:T(8,128)(2,1)} %copy.41), channel_id=1, source_target_pairs={{0,1},{1,2},{2,3},{4,5},{5,6},{6,7},{8,9},{9,10},{10,11},{12,13},{... | collective-permute-start | bytes 1769480 | tf_op jit(solution)/shard_map/ppermute | solution.py:11
  55.5 1.1 %fusion.14 = f32[2,384,384]{2,1,0:T(8,128)S(1)} fusion(bf16[2,384,384]{2,1,0:T(8,128)(2,1)S(1)} %bitcast.135, bf16[1,384,384]{2,1,0:T(8,128)(2,1)S(1)} %copy-done.3), kind=kOutput, calls=%fused_computation.29 | convolution fusion | flops 453279744 | bytes 2064384 | tf_op jit(solution)/shard_map/ceij,kj->ceik/dot_general | solution.py:39
  56.6 9.4 %collective-permute-done.1 = bf16[2,1,384,384]{3,2,0,1:T(8,128)(2,1)} collective-permute-done((bf16[2,1,384,384]{3,2,0,1:T(8,128)(2,1)}, bf16[2,1,384,384]{3,2,0,1:T(8,128)(2,1)}, u32[]{:S(2)}, u32[]{:S(2)}) %collective-permute-start.1) | collective-permute-done | bytes 589856 | tf_op jit(solution)/shard_map/ppermute | solution.py:11
  66.0 5.0 %collective-permute-done = bf16[2,1,384,384]{2,3,0,1:T(8,128)(2,1)} collective-permute-done((bf16[2,1,384,384]{2,3,0,1:T(8,128)(2,1)}, bf16[2,1,384,384]{2,3,0,1:T(8,128)(2,1)}, u32[]{:S(2)}, u32[]{:S(2)}) %collective-permute-start) | collective-permute-done | bytes 589856 | tf_op jit(solution)/shard_map/ppermute | solution.py:11
  71.0 2.3 %add_convert_fusion = bf16[2,1,384,384]{3,2,0,1:T(8,128)(2,1)S(1)} fusion(bf16[2,1,384,384]{3,2,0,1:T(8,128)(2,1)} %collective-permute-done.1, f32[2,384,384]{2,1,0:T(8,128)S(1)} %fusion.14, bf16[2,1,384,384]{2,3,0,1:T(8,128)(2,1)} %collective-permute-done, bf16[1,384,384]{2,1,0:T(8,128)(2,1)S(1)} %copy-done), kind=kOutput, calls=%fused_computation.35 | convolution fusion | flops 454459392 | bytes 3244032 | tf_op jit(solution)/shard_map/ceij,kj->ceik/dot_general | solution.py:39
  73.9 12.8 %all_to_all.28 = bf16[2,1,384,384]{3,0,1,2:T(2,128)(2,1)S(1)} all-to-all(bf16[2,1,384,384]{3,0,1,2:T(2,128)(2,1)S(1)} %copy.45), channel_id=1, replica_groups=mesh['energy'=8,'space'=4] {'energy'}, dimensions={2} | all-to-all | bytes 1179648 | tf_op jit(solution)/shard_map/all_to_all | solution.py:90
  86.7 2.9 %slice_reduce_fusion = (bf16[384,384]{1,0:T(8,128)(2,1)S(1)}, bf16[384,384]{1,0:T(8,128)(2,1)S(1)}) fusion(bf16[2,1,384,384]{3,0,1,2:T(2,128)(2,1)S(1)} %all_to_all.28), kind=kLoop, calls=%fused_computation.38 | loop fusion | bytes 1179648 | tf_op jit(solution)/shard_map/slice | solution.py:92
  92.5 1.0 %multiply_add_fusion = (f32[16,18432]{1,0:T(8,128)S(1)}, f32[16,18432]{1,0:T(8,128)S(1)}) fusion(f32[16,18432]{1,0:T(8,128)S(1)} %convolution_subtract_fusion.2, f32[16,18432]{1,0:T(8,128)S(1)} %copy-done.1, f32[16,18432]{1,0:T(8,128)S(1)} %convolution_subtract_fusion, f32[16,18432]{1,0:T(8,128)S(1)} %fusion.46, bf16[8,18432]{1,0:T(8,128)(2,1)S(1)} %squeeze.34, ...), kind=kOutput, calls=%fused_computation.34 | convolution fusion | flops 30377728 | bytes 7372832 | tf_op jit(solution)/shard_map/dot_general | solution.py:15
  94.3 0.7 fusion.42
  95.1 0.8 fusion.10
  95.9 0.7 fusion.11
  96.7 0.9 pad_maximum_fusion.1
  (41 shorter events, 11.5 us)
Async XLA Ops:
  0.0 49.0 %copy-start = (bf16[1,384,384]{2,1,0:T(8,128)(2,1)S(1)}, bf16[1,384,384]{2,1,0:T(8,128)(2,1)}, u32[]{:S(2)}) copy-start(bf16[1,384,384]{2,1,0:T(8,128)(2,1)} %param.6) | copy-start | bytes 884740
  0.0 3.9 %copy-start.2 = (bf16[4,1,1,384,384]{4,3,2,1,0:T(8,128)(2,1)S(1)}, bf16[4,1,1,384,384]{4,3,2,1,0:T(8,128)(2,1)}, u32[]{:S(2)}) copy-start(bf16[4,1,1,384,384]{4,3,2,1,0:T(8,128)(2,1)} %param.4) | copy-start | bytes 3538948
  24.4 0.7 copy-start.4
  49.0 6.6 %copy-start.3 = (bf16[1,384,384]{2,1,0:T(8,128)(2,1)S(1)}, bf16[1,384,384]{2,1,0:T(8,128)(2,1)}, u32[]{:S(2)}) copy-start(bf16[1,384,384]{2,1,0:T(8,128)(2,1)} %param.5) | copy-start | bytes 884740
  50.9 15.2 %collective-permute-start.1 = (bf16[2,1,384,384]{3,2,0,1:T(8,128)(2,1)}, bf16[2,1,384,384]{3,2,0,1:T(8,128)(2,1)}, u32[]{:S(2)}, u32[]{:S(2)}) collective-permute-start(bf16[2,1,384,384]{3,2,0,1:T(8,128)(2,1)} %fusion.17), channel_id=1, source_target_pairs={{1,0},{2,1},{3,2},{5,4},{6,5},{7,6},{9,8},{10,9},{11,10},{13,12},{... | collective-permute-start | bytes 1769480 | tf_op jit(solution)/shard_map/ppermute | solution.py:11
  54.1 16.9 %collective-permute-start = (bf16[2,1,384,384]{2,3,0,1:T(8,128)(2,1)}, bf16[2,1,384,384]{2,3,0,1:T(8,128)(2,1)}, u32[]{:S(2)}, u32[]{:S(2)}) collective-permute-start(bf16[2,1,384,384]{2,3,0,1:T(8,128)(2,1)} %copy.41), channel_id=1, source_target_pairs={{0,1},{1,2},{2,3},{4,5},{5,6},{6,7},{8,9},{9,10},{10,11},{12,13},{... | collective-permute-start | bytes 1769480 | tf_op jit(solution)/shard_map/ppermute | solution.py:11
  91.3 1.3 %copy-start.1 = (f32[16,18432]{1,0:T(8,128)S(1)}, f32[16,18432]{1,0:T(8,128)}, u32[]{:S(2)}) copy-start(f32[16,18432]{1,0:T(8,128)} %get-tuple-element.15) | copy-start | bytes 3538948
